TPU v7x, 32 devices: a whole 2x2x4 slice. The times are simulated.
32 devices in a mesh: span: 16 (over z, y, x), wall: 2 (over core).
Axes of the slice: x: 2, y: 2, z: 4, core: 2. Of those that a mesh axis runs over, the one named last changes fastest.
Arguments:
- velocity: bfloat16 [64, 3, 8, 128, 256], P(None, None, None, 'span', 'wall'), may hold values from -1080 to 1080, as said below
- wall_metric: float32 [256], P('wall'), may hold values from 0.5 to 2
Outputs:
- modes: bfloat16 [64, 3, 2, 128, 256], P(None, None, None, 'span', 'wall')
- r_factor: float32 [64, 64], replicated
Inputs may be any that keep to these rules, and one draw needn't show every extreme that they name: velocity fields of order up to a few hundred.
All inputs are finite; a program needn't handle non-finite values.
Results may differ from a plain program's by a relative error of at most 0.0063.
Values may be sent and summed in bfloat16 or wider, within the bound.
A program may use at most 64 MiB of HBM per device.

v0:
```python
import jax
import jax.numpy as jnp
from jax import lax
from jax.sharding import PartitionSpec as P


def padded_2(block, sides, width, periodic):
    for axis, dim in sides:
        count = lax.axis_size(axis)
        forward = [(i, i + 1) for i in range(count - 1)]
        if periodic:
            forward.append((count - 1, 0))
        backward = [(target, source) for source, target in forward]
        low = lax.ppermute(
            lax.slice_in_dim(block, block.shape[dim] - width, None, axis=dim), axis, forward
        )
        high = lax.ppermute(lax.slice_in_dim(block, 0, width, axis=dim), axis, backward)
        block = jnp.concatenate([low, block, high], axis=dim)
    return block


def stencil(padded, axis, length):

    def take(k):
        return lax.slice_in_dim(padded, 3 + k, 3 + k + length, axis=axis).astype(jnp.float32)

    return (45.0 * (take(1) - take(-1)) - 9.0 * (take(2) - take(-2)) + (take(3) - take(-3))) / 60.0


def factor_lower(gram):
    order = gram.shape[0]
    positions = jnp.arange(order, dtype=jnp.int32)

    def column(index, lower):
        at = jnp.asarray(index).astype(jnp.int32)
        above = lax.dynamic_slice_in_dim(gram, at, 1, 1)[:, 0]
        row_j = lax.dynamic_slice_in_dim(lower, at, 1, 0)[0]
        rest = above - jnp.sum(lower * row_j[None, :], axis=1)
        pivot = jnp.sqrt(lax.dynamic_slice_in_dim(rest, at, 1, 0)[0])
        keep = (positions >= at).astype(gram.dtype)
        pick = (positions == at).astype(gram.dtype)
        return lower + (keep * rest / pivot)[:, None] * pick[None, :]

    return lax.fori_loop(0, order, column, jnp.zeros_like(gram))


def invert_lower(lower):
    order = lower.shape[0]
    positions = jnp.arange(order, dtype=jnp.int32)

    def row_step(index, inverse):
        at = jnp.asarray(index).astype(jnp.int32)
        pick = (positions == at).astype(lower.dtype)
        row_l = lax.dynamic_slice_in_dim(lower, at, 1, 0)[0]
        pivot = lax.dynamic_slice_in_dim(row_l, at, 1, 0)[0]
        new_row = (pick - jnp.sum(row_l[:, None] * inverse, axis=0)) / pivot
        return inverse + pick[:, None] * new_row[None, :]

    return lax.fori_loop(0, order, row_step, jnp.zeros_like(lower))


def per_device(velocity, wall_metric):
    snaps = velocity.shape[0]
    planes = velocity.shape[2] - 6
    span_cells = velocity.shape[3]
    wall_cells = velocity.shape[4]
    inner = velocity[:, :, 3 : 3 + planes]
    span_padded = padded_2(inner, (("span", 3),), 3, True)
    wall_padded = padded_2(inner, (("wall", 4),), 3, False)
    du_dz = stencil(span_padded[:, 0], 2, span_cells)
    dv_dz = stencil(span_padded[:, 1], 2, span_cells)
    du_dy = wall_metric * stencil(wall_padded[:, 0], 3, wall_cells)
    dw_dy = wall_metric * stencil(wall_padded[:, 2], 3, wall_cells)
    dv_dx = stencil(velocity[:, 1], 1, planes)
    dw_dx = stencil(velocity[:, 2], 1, planes)
    vorticity = jnp.stack([dw_dy - dv_dz, du_dz - dw_dx, dv_dx - du_dy], axis=1).astype(
        jnp.bfloat16
    )
    flat = vorticity.reshape(snaps, -1)
    partial_gram = jnp.dot(flat, flat.T, preferred_element_type=jnp.float32)
    summed = lax.psum(partial_gram, ("span", "wall"))
    total_rows = (
        3 * planes * span_cells * lax.axis_size("span") * wall_cells * lax.axis_size("wall")
    )
    gram = summed / total_rows
    lower = factor_lower(gram)
    upper = lower.T
    r_inverse = invert_lower(lower).T.astype(jnp.bfloat16)
    modes = jnp.dot(r_inverse.T, flat, preferred_element_type=jnp.float32).astype(jnp.bfloat16)
    return (modes.reshape(vorticity.shape), upper)


def solution(mesh):
    in_specs = (P(None, None, None, "span", "wall"), P("wall"))
    out_specs = (P(None, None, None, "span", "wall"), P())
    return jax.shard_map(
        per_device, mesh=mesh, in_specs=in_specs, out_specs=out_specs, check_vma=False
    )
```

profile of v0, /device:TPU:0, one launch (start us, length us, event | category | flops | bytes accessed | tf_op | source)
XLA Modules:
  0.0 268.7 jit_solution(13451744703677940746)
XLA Ops:
  0.6 1.8 fusion.11
  2.4 0.8 copy.39
  3.2 2.9 %collective-permute-start.2 = (bf16[64,3,2,3,128]{4,0,3,2,1:T(8,128)(2,1)}, bf16[64,3,2,3,128]{4,0,3,2,1:T(8,128)(2,1)}, u32[]{:S(2)}, u32[]{:S(2)}) collective-permute-start(bf16[64,3,2,3,128]{4,0,3,2,1:T(8,128)(2,1)} %copy.39), channel_id=1, source_target_pairs={{0,2},{2,4},{4,6},{6,8},{8,10},{10,12},{12,14},{14,16},{16,18},{18... | collective-permute-start | bytes 884744 | tf_op jit(solution)/shard_map/ppermute | solution.py:14
  6.2 3.0 %fusion.13 = (bf16[64,3,2,8,3]{4,3,2,1,0:T(8,128)(2,1)}, bf16[64,3,2,8,3]{4,3,2,1,0:T(8,128)(2,1)}) fusion(bf16[64,3,8,8,128]{4,3,2,1,0:T(8,128)(2,1)} %param.6), kind=kLoop, calls=%fused_computation.43 | loop fusion | bytes 73728 | tf_op jit(solution)/shard_map/slice | solution.py:15
  9.1 2.4 copy.36
  11.5 2.1 collective-permute-start
  13.6 2.4 copy.38
  16.0 1.3 collective-permute-start.1
  17.3 0.8 copy.40
  18.1 4.3 %collective-permute-start.3 = (bf16[64,3,2,3,128]{4,0,3,2,1:T(8,128)(2,1)}, bf16[64,3,2,3,128]{4,0,3,2,1:T(8,128)(2,1)S(1)}, u32[]{:S(2)}, u32[]{:S(2)}) collective-permute-start(bf16[64,3,2,3,128]{4,0,3,2,1:T(8,128)(2,1)} %copy.40), channel_id=1, source_target_pairs={{2,0},{4,2},{6,4},{8,6},{10,8},{12,10},{14,12},{16,14},{18,16},{20... | collective-permute-start | bytes 884744 | tf_op jit(solution)/shard_map/ppermute | solution.py:17
  22.6 2.7 copy_bitcast_fusion
  25.3 1.3 copy.26
  26.5 1.2 copy.27
  27.8 1.0 constant_dynamic-update-slice_fusion.2
  31.4 0.7 subtract_bitcast_fusion
  34.0 40.6 %psum.7 = f32[64,64]{1,0:T(8,128)S(1)} all-reduce(f32[64,64]{1,0:T(8,128)S(1)} %convolution_bitcast_fusion), channel_id=1, replica_groups=mesh['span'=16,'wall'=2] {'span','wall'}, use_global_device_ids=true, to_apply=%region_0.0 | all-reduce | flops 4096 | bytes 32768 | tf_op jit(solution)/shard_map/psum | solution.py:81
  74.6 99.4 %while.33 = (s32[]{:T(128)}, f32[64,64]{1,0:T(8,128)S(1)}, f32[64,64]{0,1:T(8,128)S(1)}, s32[]{:T(128)}, s32[]{:T(128)}) while((s32[]{:T(128)}, f32[64,64]{1,0:T(8,128)S(1)}, f32[64,64]{0,1:T(8,128)S(1)}, s32[]{:T(128)}, s32[]{:T(128)}) %tuple.87), condition=%wide.region_3.0_spmd.clone.clone, body=%wide.region_1.0_spmd.clone.clone.sunk | while | flops 29059 | bytes 86889 | solution.py:44
  174.0 0.7 copy.34
  174.7 92.6 %while.32 = (s32[]{:T(128)}, f32[64,64]{1,0:T(8,128)S(1)}, f32[64,64]{1,0:T(8,128)S(1)}, s32[]{:T(128)}, s32[]{:T(128)}, /*index=5*/s32[]{:T(128)}) while((s32[]{:T(128)}, f32[64,64]{1,0:T(8,128)S(1)}, f32[64,64]{1,0:T(8,128)S(1)}, s32[]{:T(128)}, s32[]{:T(128)}, /*index=5*/s32[]{:T(128)}) %tuple.90), condition=%wide.region_6.0_spmd.clone, body=%wide.region_4.0_spmd.clone.sunk | while | flops 24900 | bytes 51580 | solution.py:59
  175.4 0.6 subtract_divide_fusion.2
  176.9 0.6 subtract_divide_fusion.2
  178.3 0.6 subtract_divide_fusion.2
  179.8 0.6 subtract_divide_fusion.2
  181.2 0.6 subtract_divide_fusion.2
  182.7 0.6 subtract_divide_fusion.2
  184.1 0.6 subtract_divide_fusion.2
  185.5 0.6 subtract_divide_fusion.2
  187.0 0.6 subtract_divide_fusion.2
  188.4 0.6 subtract_divide_fusion.2
  189.9 0.6 subtract_divide_fusion.2
  191.3 0.6 subtract_divide_fusion.2
  192.8 0.6 subtract_divide_fusion.2
  194.2 0.6 subtract_divide_fusion.2
  195.7 0.6 subtract_divide_fusion.2
  197.1 0.6 subtract_divide_fusion.2
  198.6 0.6 subtract_divide_fusion.2
  200.0 0.6 subtract_divide_fusion.2
  201.5 0.6 subtract_divide_fusion.2
  202.9 0.6 subtract_divide_fusion.2
  204.4 0.6 subtract_divide_fusion.2
  205.8 0.6 subtract_divide_fusion.2
  207.3 0.6 subtract_divide_fusion.2
  208.7 0.6 subtract_divide_fusion.2
  210.1 0.6 subtract_divide_fusion.2
  211.6 0.6 subtract_divide_fusion.2
  213.0 0.6 subtract_divide_fusion.2
  214.5 0.6 subtract_divide_fusion.2
  215.9 0.6 subtract_divide_fusion.2
  217.4 0.6 subtract_divide_fusion.2
  218.8 0.6 subtract_divide_fusion.2
  220.3 0.6 subtract_divide_fusion.2
  221.7 0.6 subtract_divide_fusion.2
  223.2 0.6 subtract_divide_fusion.2
  227.5 0.6 subtract_divide_fusion.2
  229.0 0.6 subtract_divide_fusion.2
  230.4 0.6 subtract_divide_fusion.2
  240.5 0.6 subtract_divide_fusion.2
  242.0 0.6 subtract_divide_fusion.2
  243.4 0.6 subtract_divide_fusion.2
  244.9 0.6 subtract_divide_fusion.2
  255.0 0.6 subtract_divide_fusion.2
  256.4 0.6 subtract_divide_fusion.2
  257.9 0.6 subtract_divide_fusion.2
  267.7 1.0 copy.44
  (882 shorter events, 120.2 us)
Async XLA Ops:
  3.2 24.5 %collective-permute-start.2 = (bf16[64,3,2,3,128]{4,0,3,2,1:T(8,128)(2,1)}, bf16[64,3,2,3,128]{4,0,3,2,1:T(8,128)(2,1)}, u32[]{:S(2)}, u32[]{:S(2)}) collective-permute-start(bf16[64,3,2,3,128]{4,0,3,2,1:T(8,128)(2,1)} %copy.39), channel_id=1, source_target_pairs={{0,2},{2,4},{4,6},{6,8},{8,10},{10,12},{12,14},{14,16},{16,18},{18... | collective-permute-start | bytes 884744 | tf_op jit(solution)/shard_map/ppermute | solution.py:14
  6.2 16.2 %copy-start = (bf16[64,3,8,8,128]{4,3,2,1,0:T(8,128)(2,1)S(1)}, bf16[64,3,8,8,128]{4,3,2,1,0:T(8,128)(2,1)}, u32[]{:S(2)}) copy-start(bf16[64,3,8,8,128]{4,3,2,1,0:T(8,128)(2,1)} %param.6) | copy-start | bytes 9437188
  11.5 13.7 %collective-permute-start = (bf16[64,3,2,8,3]{0,3,4,2,1:T(8,128)(2,1)}, bf16[64,3,2,8,3]{0,3,4,2,1:T(8,128)(2,1)}, u32[]{:S(2)}, u32[]{:S(2)}) collective-permute-start(bf16[64,3,2,8,3]{0,3,4,2,1:T(8,128)(2,1)} %copy.36), channel_id=1, source_target_pairs={{0,1},{2,3},{4,5},{6,7},{8,9},{10,11},{12,13},{14,15},{16,17},{18,... | collective-permute-start | bytes 55304 | tf_op jit(solution)/shard_map/ppermute | solution.py:14
  16.0 10.5 %collective-permute-start.1 = (bf16[64,3,2,8,3]{0,3,4,2,1:T(8,128)(2,1)}, bf16[64,3,2,8,3]{0,3,4,2,1:T(8,128)(2,1)}, u32[]{:S(2)}, u32[]{:S(2)}) collective-permute-start(bf16[64,3,2,8,3]{0,3,4,2,1:T(8,128)(2,1)} %copy.38), channel_id=1, source_target_pairs={{1,0},{3,2},{5,4},{7,6},{9,8},{11,10},{13,12},{15,14},{17,16},{19,... | collective-permute-start | bytes 55304 | tf_op jit(solution)/shard_map/ppermute | solution.py:17
  18.1 11.3 %collective-permute-start.3 = (bf16[64,3,2,3,128]{4,0,3,2,1:T(8,128)(2,1)}, bf16[64,3,2,3,128]{4,0,3,2,1:T(8,128)(2,1)S(1)}, u32[]{:S(2)}, u32[]{:S(2)}) collective-permute-start(bf16[64,3,2,3,128]{4,0,3,2,1:T(8,128)(2,1)} %copy.40), channel_id=1, source_target_pairs={{2,0},{4,2},{6,4},{8,6},{10,8},{12,10},{14,12},{16,14},{18,16},{20... | collective-permute-start | bytes 884744 | tf_op jit(solution)/shard_map/ppermute | solution.py:17
  22.5 2.7 %copy-start.3 = (f32[128]{0:T(128)S(1)}, f32[128]{0:T(128)}, u32[]{:S(2)}) copy-start(f32[128]{0:T(128)} %param.7) | copy-start | bytes 1540
  25.2 3.5 %slice-start = ((bf16[64,3,8,8,128]{4,3,2,1,0:T(8,128)(2,1)}), bf16[64,3,2,8,128]{4,3,2,1,0:T(8,128)(2,1)S(1)}, s32[]{:S(2)}) async-start(bf16[64,3,8,8,128]{4,3,2,1,0:T(8,128)(2,1)} %param.6), calls=%async_computation | async-start | bytes 1572864 | tf_op jit(solution)/shard_map/slice | solution.py:67
  30.1 1.2 copy-start.1
  31.3 1.2 copy-start.2
where the time goes:
time: 270 us; the launch traced here: 269 us
  local copies, waits for them, and re-layouts  98 us (36%)
  other arithmetic  69.6 us (26%)
  loops' own time  48.4 us (18%)
  blocking collectives  40.6 us (15%)
  starting transfers between devices  10.6 us (4%)
    another operation x1, loops' own time, factor_lower(): return lax.fori_loop(0, order, column, jnp.zeros_like(gram))  46.6 us
    div x64, other arithmetic, row_step(): new_row = (pick - jnp.sum(row_l[:, None] * inverse, axis=0)) / pivot  41.5 us
    psum x1, blocking collectives, per_device(): summed = lax.psum(partial_gram, ('span', 'wall'))  40.6 us
    dynamic_slice x64, local copies, waits for them, and re-layouts, column(): pivot = jnp.sqrt(lax.dynamic_slice_in_dim(rest, at, 1, 0)[0])  37.7 us
    dynamic_slice x64, local copies, waits for them, and re-layouts, row_step(): pivot = lax.dynamic_slice_in_dim(row_l, at, 1, 0)[0]  37.7 us
    unnamed x16, local copies, waits for them, and re-layouts  10.1 us
    reduce_sum x64, other arithmetic, column(): rest = above - jnp.sum(lower * row_j[None, :], axis=1)  6.84 us
    reduce_sum x64, other arithmetic, row_step(): new_row = (pick - jnp.sum(row_l[:, None] * inverse, axis=0)) / pivot  6.03 us
  transfers between devices with their start and end apart: 4, of which 1 were waited for; matrix products, arithmetic and copies ran while one was open for 6% of the time, Pallas kernels for 0%

commit v1 on v0

v1 whole, which is shorter than its diff:
```python
import functools

import jax
import jax.numpy as jnp
import ml_dtypes
import numpy as np
from jax import lax
from jax.experimental import pallas as pl
from jax.experimental.pallas import tpu as pltpu
from jax.sharding import PartitionSpec as P

MESH = pl.DeviceIdType.MESH
BF = jnp.bfloat16
F32 = jnp.float32


def coef(offset):
    table = {1: 45.0, 2: -9.0, 3: 1.0}
    size = np.abs(offset)
    out = np.zeros(offset.shape, np.float32)
    for step, value in table.items():
        out = np.where(size == step, value * np.sign(offset), out)
    return out


def constants(snaps, cells, lanes, planes, block):
    groups = block * planes
    z = np.arange(cells)
    r = np.arange(3)
    eye = np.eye(groups, dtype=np.float32)
    pick = np.stack(
        [
            np.kron(eye, (z[None, :] == r[:, None]).astype(np.float32)),
            np.kron(eye, (z[None, :] == cells - 3 + r[:, None]).astype(np.float32)),
        ]
    )
    span = np.concatenate(
        [
            np.kron(eye, coef(z[None, :] - z[:, None])),
            np.kron(eye, coef(r[None, :] - 3 - z[:, None])),
            np.kron(eye, coef(cells + r[None, :] - z[:, None])),
        ],
        axis=1,
    )
    y = np.arange(lanes)
    diff = y[:, None] - y[None, :]
    wall = np.concatenate([coef(diff), coef(diff - lanes), coef(diff + lanes)], axis=0)
    owner = np.arange(snaps * cells) // cells
    one = (owner[:, None] == np.arange(snaps)[None, :]).astype(np.float32)
    fold = np.concatenate([one, one], axis=1)
    spread = np.concatenate([np.zeros_like(one.T), one.T], axis=0)
    return [jnp.asarray(a.astype(ml_dtypes.bfloat16)) for a in (pick, span, wall, fold, spread)]


def dot(a, b):
    return jnp.dot(a, b, preferred_element_type=F32)


def eliminate(rows):
    groups = list(rows)
    count = len(groups)
    sub = lax.broadcasted_iota(jnp.int32, (8, 128), 0)
    for j in range(8 * count):
        b, r = divmod(j, 8)
        pivot_row = jnp.broadcast_to(groups[b][r : r + 1, :], (8, 128))
        inv = 1.0 / jnp.broadcast_to(pivot_row[:, j : j + 1], (8, 128))
        scaled = pivot_row * inv
        for i in range(b, count):
            if i == b and r == 7:
                continue
            column = jnp.broadcast_to(groups[i][:, j : j + 1], (8, 128))
            if i == b:
                column = jnp.where(sub > r, column, 0.0)
            groups[i] = groups[i] - column * scaled
    return groups


def kernel(
    span_count, wall_count, total_rows,
    vel, metric_ref, pick_ref, span_ref, wall_ref, fold_ref, spread_ref,
    out_ref, r_ref,
    u_buf, vw_buf, send_buf, lo_buf, hi_buf, ylo_buf, yhi_buf, acc, vort, prod,
    wall_sum, span_sum,
    local_sem, hs_sem, hr_sem, ys_sem, yr_sem, ws_sem, wr_sem, ss_sem, sr_sem,
):
    snaps = vel.shape[0]
    planes = u_buf.shape[1]
    cells, lanes = vel.shape[3], vel.shape[4]
    block = 16
    rows = block * planes * cells
    edge = block * planes * 3
    blocks = snaps // block
    me = lax.axis_index("span")
    mw = lax.axis_index("wall")

    load_u = pltpu.make_async_copy(vel.at[:, 0, pl.ds(3, planes)], u_buf, local_sem.at[0])
    load_v = pltpu.make_async_copy(vel.at[:, 1], vw_buf.at[0], local_sem.at[1])
    load_w = pltpu.make_async_copy(vel.at[:, 2], vw_buf.at[1], local_sem.at[2])
    load_u.start()
    load_v.start()
    load_w.start()

    barrier = pltpu.get_barrier_semaphore()
    for d in range(1, span_count):
        pl.semaphore_signal(
            barrier, inc=1, device_id=(lax.rem(me + d, span_count), mw), device_id_type=MESH
        )
    for d in range(1, wall_count):
        pl.semaphore_signal(
            barrier, inc=1, device_id=(me, lax.rem(mw + d, wall_count)), device_id_type=MESH
        )

    def inner(c, k):
        at = pl.ds(k * block, block)
        if c == 0:
            value = u_buf[at]
        else:
            value = vw_buf[c - 1, at, pl.ds(3, planes)]
        return value.astype(F32).reshape(rows, lanes).astype(BF)

    load_u.wait()
    load_v.wait()
    for c in range(2):
        for k in range(blocks):
            f = inner(c, k)
            for side in range(2):
                send_buf[side, c, k * edge : (k + 1) * edge] = dot(pick_ref[side], f).astype(BF)
    load_w.wait()
    pl.semaphore_wait(barrier, span_count + wall_count - 2)

    down = lax.rem(me + span_count - 1, span_count)
    up = lax.rem(me + 1, span_count)
    halo = []
    for c in range(2):
        to_down = pltpu.make_async_remote_copy(
            send_buf.at[0, c], hi_buf.at[c], hs_sem.at[0, c], hr_sem.at[0, c],
            device_id=(down, mw), device_id_type=MESH,
        )
        to_up = pltpu.make_async_remote_copy(
            send_buf.at[1, c], lo_buf.at[c], hs_sem.at[1, c], hr_sem.at[1, c],
            device_id=(up, mw), device_id_type=MESH,
        )
        to_down.start()
        to_up.start()
        halo.append((to_down, to_up))

    wall_src = (u_buf, vw_buf.at[1, :, pl.ds(3, planes)])
    y_up = [
        pltpu.make_async_remote_copy(
            wall_src[c], ylo_buf.at[c], ys_sem.at[0, c], yr_sem.at[0, c],
            device_id=(me, lax.rem(mw + 1, wall_count)), device_id_type=MESH,
        )
        for c in range(2)
    ]
    y_down = [
        pltpu.make_async_remote_copy(
            wall_src[c], yhi_buf.at[c], ys_sem.at[1, c], yr_sem.at[1, c],
            device_id=(me, lax.rem(mw + wall_count - 1, wall_count)), device_id_type=MESH,
        )
        for c in range(2)
    ]

    @pl.when(mw < wall_count - 1)
    def _():
        for c in range(2):
            y_up[c].start()

    @pl.when(mw > 0)
    def _():
        for c in range(2):
            y_down[c].start()

    @pl.when(mw == 0)
    def _():
        ylo_buf[...] = jnp.zeros_like(ylo_buf)

    @pl.when(mw == wall_count - 1)
    def _():
        yhi_buf[...] = jnp.zeros_like(yhi_buf)

    def along_x(k, carry):
        at = pl.ds(k * 4, 4)
        for c in range(2):
            f = [vw_buf[c, at, q].astype(F32) for q in range(6 + planes)]
            for p in range(planes):
                d = (
                    45.0 * (f[p + 4] - f[p + 2]) - 9.0 * (f[p + 5] - f[p + 1])
                    + (f[p + 6] - f[p])
                )
                if c == 0:
                    acc[2, p, at] = d
                else:
                    acc[1, p, at] = -d
        return carry

    lax.fori_loop(0, snaps // 4, along_x, 0)

    @pl.when(mw > 0)
    def _():
        for c in range(2):
            y_up[c].wait_recv()

    @pl.when(mw < wall_count - 1)
    def _():
        for c in range(2):
            y_down[c].wait_recv()

    metric = metric_ref[...].reshape(1, 1, 1, lanes)
    for c in range(2):
        for k in range(blocks):
            at = pl.ds(k * block, block)
            f = inner(2 * c, k)
            low = ylo_buf[c, at].astype(F32).reshape(rows, lanes).astype(BF)
            high = yhi_buf[c, at].astype(F32).reshape(rows, lanes).astype(BF)
            d = dot(jnp.concatenate([f, low, high], axis=1), wall_ref[...])
            d = d.reshape(block, planes, cells, lanes) * metric
            for p in range(planes):
                if c == 0:
                    acc[2, p, at] = acc[2, p, at] - d[:, p]
                else:
                    acc[0, p, at] = d[:, p]

    def finish(comp, p, k, value):
        slab = comp * planes + p
        vort[k * block * cells : (k + 1) * block * cells, slab * lanes : (slab + 1) * lanes] = (
            (value * (1.0 / 60.0)).reshape(block * cells, lanes).astype(BF)
        )

    for k in range(blocks):
        at = pl.ds(k * block, block)
        for p in range(planes):
            finish(2, p, k, acc[2, p, at])
    for c in range(2):
        halo[c][0].wait_recv()
        halo[c][1].wait_recv()
        for k in range(blocks):
            at = pl.ds(k * block, block)
            part = slice(k * edge, (k + 1) * edge)
            stack = jnp.concatenate([inner(c, k), lo_buf[c, part], hi_buf[c, part]], axis=0)
            d = dot(span_ref[...], stack).reshape(block, planes, cells, lanes)
            for p in range(planes):
                if c == 0:
                    finish(1, p, k, acc[1, p, at] + d[:, p])
                else:
                    finish(0, p, k, acc[0, p, at] - d[:, p])

    wide = snaps * cells
    tiles = wide // 128
    lane_z = lax.rem(lax.broadcasted_iota(jnp.int32, (snaps, 128), 1), cells)
    parts = []
    for t in range(tiles):
        prod[t] = lax.dot_general(
            vort[...], vort[t * 128 : (t + 1) * 128],
            (((1,), (1,)), ((), ())), preferred_element_type=F32,
        )
        q = jnp.zeros((snaps, 128), F32)
        for z in range(cells):
            q = jnp.where(lane_z == z, prod[t, pl.ds(z, snaps, stride=cells), :], q)
        parts.append(q)
    q = jnp.concatenate(parts, axis=1)
    q1 = q.astype(BF)
    rest = q - q1.astype(F32)
    q2 = rest.astype(BF)
    q3 = (rest - q2.astype(F32)).astype(BF)
    g3 = dot(jnp.concatenate([q1, q2, q3], axis=0), fold_ref[...])
    g = g3[:snaps] + g3[snaps : 2 * snaps] + g3[2 * snaps :]
    half = snaps // 2
    lane = lax.broadcasted_iota(jnp.int32, (half, 2 * snaps), 1)
    packed = jnp.where(lane < snaps, g[:half], g[half:])

    wall_sum[mw] = packed
    copies = []
    for d in range(1, wall_count):
        copy = pltpu.make_async_remote_copy(
            wall_sum.at[mw], wall_sum.at[mw], ws_sem.at[d], wr_sem.at[d],
            device_id=(me, lax.rem(mw + d, wall_count)), device_id_type=MESH,
        )
        copy.start()
        copies.append(copy)
    for copy in copies:
        copy.wait_recv()
    total = wall_sum[0]
    for i in range(1, wall_count):
        total = total + wall_sum[i]
    span_sum[me] = total
    for d in range(1, span_count):
        copy = pltpu.make_async_remote_copy(
            span_sum.at[me], span_sum.at[me], ss_sem.at[d], sr_sem.at[d],
            device_id=(lax.rem(me + d, span_count), mw), device_id_type=MESH,
        )
        copy.start()
        copies.append(copy)
    for copy in copies[wall_count - 1 :]:
        copy.wait_recv()
    total = span_sum[0]
    for i in range(1, span_count):
        total = total + span_sum[i]
    gram = total / total_rows

    sub = lax.broadcasted_iota(jnp.int32, (half, 2 * snaps), 0)
    top = jnp.where(lane < snaps, gram, (lane - snaps == sub).astype(F32))
    bottom = jnp.where(
        lane < snaps, pltpu.roll(gram, snaps, 1), (lane - snaps - half == sub).astype(F32)
    )
    groups = [top[8 * i : 8 * i + 8] for i in range(half // 8)]
    groups += [bottom[8 * i : 8 * i + 8] for i in range(half // 8)]
    done = jnp.concatenate(eliminate(groups), axis=0)
    lane = lax.broadcasted_iota(jnp.int32, (snaps, 2 * snaps), 1)
    sub = lax.broadcasted_iota(jnp.int32, (snaps, 2 * snaps), 0)
    diagonal = jnp.sum(jnp.where(lane == sub, done, 0.0), axis=1, keepdims=True)
    done = jnp.where(lane < sub, 0.0, done / jnp.sqrt(diagonal))
    r_ref[...] = done[:, :snaps]

    x = dot(done.astype(BF), spread_ref[...]).astype(BF)
    full = dot(fold_ref[:, :snaps], x)
    row_z = lax.rem(lax.broadcasted_iota(jnp.int32, (wide, wide), 0), cells)
    col_z = lax.rem(lax.broadcasted_iota(jnp.int32, (wide, wide), 1), cells)
    weights = jnp.where(row_z == col_z, full, 0.0).astype(BF)
    for comp in range(3):
        for p in range(planes):
            slab = comp * planes + p
            m = dot(weights, vort[:, slab * lanes : (slab + 1) * lanes])
            out_ref[:, comp, p] = m.reshape(snaps, cells, lanes).astype(BF)

    for copy in copies:
        copy.wait_send()
    for pair in halo:
        for copy in pair:
            copy.wait_send()

    @pl.when(mw < wall_count - 1)
    def _():
        for c in range(2):
            y_up[c].wait_send()

    @pl.when(mw > 0)
    def _():
        for c in range(2):
            y_down[c].wait_send()


def per_device(velocity, wall_metric):
    snaps, comps, depth, cells, lanes = velocity.shape
    planes = depth - 6
    spans, walls = lax.axis_size("span"), lax.axis_size("wall")
    total_rows = 3 * planes * cells * spans * lanes * walls
    consts = constants(snaps, cells, lanes, planes, 16)
    vmem = pl.BlockSpec(memory_space=pltpu.VMEM)
    dma = pltpu.SemaphoreType.DMA
    edge = snaps * planes * 3
    wide = snaps * cells
    return pl.pallas_call(
        functools.partial(kernel, spans, walls, total_rows),
        out_shape=(
            jax.ShapeDtypeStruct((snaps, 3, planes, cells, lanes), BF),
            jax.ShapeDtypeStruct((snaps, snaps), F32),
        ),
        in_specs=[pl.BlockSpec(memory_space=pl.ANY)] + [vmem] * 6,
        out_specs=(vmem, vmem),
        scratch_shapes=[
            pltpu.VMEM((snaps, planes, cells, lanes), BF),
            pltpu.VMEM((2, snaps, depth, cells, lanes), BF),
            pltpu.VMEM((2, 2, edge, lanes), BF),
            pltpu.VMEM((2, edge, lanes), BF),
            pltpu.VMEM((2, edge, lanes), BF),
            pltpu.VMEM((2, snaps, planes, cells, lanes), BF),
            pltpu.VMEM((2, snaps, planes, cells, lanes), BF),
            pltpu.VMEM((3, planes, snaps, cells, lanes), F32),
            pltpu.VMEM((wide, 3 * planes * lanes), BF),
            pltpu.VMEM((wide // 128, wide, 128), F32),
            pltpu.VMEM((walls, snaps // 2, 2 * snaps), F32),
            pltpu.VMEM((spans, snaps // 2, 2 * snaps), F32),
            dma((3,)),
            dma((2, 2)),
            dma((2, 2)),
            dma((2, 2)),
            dma((2, 2)),
            dma((walls,)),
            dma((walls,)),
            dma((spans,)),
            dma((spans,)),
        ],
        compiler_params=pltpu.CompilerParams(
            collective_id=0, has_side_effects=True, vmem_limit_bytes=48 << 20
        ),
        name="pod",
    )(velocity, wall_metric.reshape(1, lanes), *consts)


def solution(mesh):
    in_specs = (P(None, None, None, "span", "wall"), P("wall"))
    out_specs = (P(None, None, None, "span", "wall"), P())
    return jax.shard_map(
        per_device, mesh=mesh, in_specs=in_specs, out_specs=out_specs, check_vma=False
    )
```

time: 270 us -> 43.8 us (0.16)
  local copies, waits for them, and re-layouts: 98 us -> 8.57 us
  other arithmetic: 69.6 us -> 0 us
  loops' own time: 48.4 us -> 0 us
  blocking collectives: 40.6 us -> 0 us
  Pallas kernels: 0 us -> 34.3 us
  starting transfers between devices: 10.6 us -> 0 us
    dynamic_slice x128 -> x0, local copies, waits for them, and re-layouts: 75.4 us -> none  [the longest x64 37.7 us: column(): pivot = jnp.sqrt(lax.dynamic_slice_in_dim(rest, at, 1, 0)[0])]
    another operation x2 -> x0, loops' own time: 48.4 us -> none  [the longest x1 46.6 us: factor_lower(): return lax.fori_loop(0, order, column, jnp.zeros_like(gram))]
    div x65 -> x0, other arithmetic: 41.5 us -> none  [the longest x64 41.5 us: row_step(): new_row = (pick - jnp.sum(row_l[:, None] * inverse, axis=0)) / pivot]
    psum x1 -> x0, blocking collectives: 40.6 us -> none  [per_device(): summed = lax.psum(partial_gram, ('span', 'wall'))]
    pallas_call x0 -> x1, Pallas kernels: none -> 34.3 us  [per_device(): pl.pallas_call(functools.partial(kernel, spans, walls, total_rows), out_s...]
    reduce_sum x128 -> x0, other arithmetic: 12.9 us -> none  [the longest x64 6.84 us: column(): rest = above - jnp.sum(lower * row_j[None, :], axis=1)]
    ppermute x4 -> x0, starting transfers between devices: 10.6 us -> none  [the longest x2 5.56 us: padded_2(): lax.ppermute(lax.slice_in_dim(block, 0, width, axis=dim), axis, backward)]
    add x128 -> x0, other arithmetic: 9.97 us -> none  [the longest x64 4.99 us: column(): return lower + (keep * rest / pivot)[:, None] * pick[None, :]]
  transfers between devices with their start and end apart: 4 -> 0, of which waited for: 1 -> 0; matrix products, arithmetic and copies ran while one was open for 6% -> 0% of each run, Pallas kernels for 0% -> 0%
where the time goes in v1:
time: 43.8 us; the launch traced here: 43.5 us
  Pallas kernels  34.3 us (78%)
  local copies, waits for them, and re-layouts  8.57 us (20%)
  between operations  0.65 us (1%)
    pallas_call x1, Pallas kernels, per_device(): pl.pallas_call(functools.partial(kernel, spans, walls, total_rows), out_s...  34.3 us
    unnamed x16, local copies, waits for them, and re-layouts  8.57 us

profile of v1, /device:TPU:0, one launch (start us, length us, event | category | flops | bytes accessed | tf_op | source)
XLA Modules:
  0.0 43.5 jit_solution(2753956010150135483)
XLA Ops:
  0.6 0.0 copy-start
  0.6 1.9 %copy-done = bf16[64,3,8,8,128]{4,3,2,1,0:T(8,128)(2,1)S(1)} copy-done((bf16[64,3,8,8,128]{4,3,2,1,0:T(8,128)(2,1)S(1)}, bf16[64,3,8,8,128]{4,3,2,1,0:T(8,128)(2,1)}, u32[]{:S(2)}) %copy-start) | copy-done | bytes 3145752
  2.5 0.0 copy-start.1
  2.5 0.9 %copy-done.1 = bf16[256,448]{1,0:T(8,128)(2,1)S(1)} copy-done((bf16[256,448]{1,0:T(8,128)(2,1)S(1)}, bf16[256,448]{1,0:T(8,128)(2,1)}, u32[]{:S(2)}) %copy-start.1) | copy-done | bytes 229400
  3.5 0.0 copy-start.2
  3.5 0.9 %copy-done.2 = bf16[128,512]{1,0:T(8,128)(2,1)S(1)} copy-done((bf16[128,512]{1,0:T(8,128)(2,1)S(1)}, bf16[128,512]{1,0:T(8,128)(2,1)}, u32[]{:S(2)}) %copy-start.2) | copy-done | bytes 131096
  4.4 0.0 copy-start.3
  4.4 0.9 %copy-done.3 = bf16[512,128]{1,0:T(8,128)(2,1)S(1)} copy-done((bf16[512,128]{1,0:T(8,128)(2,1)S(1)}, bf16[512,128]{1,0:T(8,128)(2,1)}, u32[]{:S(2)}) %copy-start.3) | copy-done | bytes 131096
  5.3 0.0 copy-start.4
  5.3 0.9 %copy-done.4 = bf16[384,128]{1,0:T(8,128)(2,1)S(1)} copy-done((bf16[384,128]{1,0:T(8,128)(2,1)S(1)}, bf16[384,128]{1,0:T(8,128)(2,1)}, u32[]{:S(2)}) %copy-start.4) | copy-done | bytes 98328
  6.2 0.0 copy-start.5
  6.2 0.9 %copy-done.5 = bf16[2,96,256]{2,1,0:T(8,128)(2,1)S(1)} copy-done((bf16[2,96,256]{2,1,0:T(8,128)(2,1)S(1)}, bf16[2,96,256]{2,1,0:T(8,128)(2,1)}, u32[]{:S(2)}) %copy-start.5) | copy-done | bytes 98328
  7.1 0.0 copy-start.6
  7.1 0.7 %copy-done.6 = f32[128]{0:T(128)S(1)} copy-done((f32[128]{0:T(128)S(1)}, f32[128]{0:T(128)}, u32[]{:S(2)}) %copy-start.6) | copy-done | bytes 536
  7.7 34.3 %pod.1 = (bf16[64,3,2,8,128]{4,3,2,1,0:T(8,128)(2,1)S(1)}, f32[64,64]{1,0:T(8,128)S(1)}) custom-call(bf16[64,3,8,8,128]{4,3,2,1,0:T(8,128)(2,1)S(1)} %copy-done, f32[1,128]{1,0:T(1,128)S(1)} %bitcast.1, bf16[2,96,256]{2,1,0:T(8,128)(2,1)S(1)} %copy-done.5, bf16[256,448]{1,0:T(8,128)(2,1)S(1)} %copy-done.1, bf16[384,128]{1,0:T(8,128)(2,1)S(1)} %copy-done.4, ...), custom_call_target="tpu_custom_call" | custom-call | tf_op jit(solution)/shard_map/pod/pallas_call | solution.py:352
  42.0 0.9 %copy.11 = bf16[64,3,2,8,128]{4,3,2,1,0:T(8,128)(2,1)} copy(bf16[64,3,2,8,128]{4,3,2,1,0:T(8,128)(2,1)S(1)} %get-tuple-element.4) | data formatting | bytes 1572864
  42.9 0.6 %copy.12 = f32[64,64]{1,0:T(8,128)} copy(f32[64,64]{1,0:T(8,128)S(1)} %get-tuple-element.5) | data formatting | bytes 32768
Async XLA Ops:
  0.6 1.9 %copy-start = (bf16[64,3,8,8,128]{4,3,2,1,0:T(8,128)(2,1)S(1)}, bf16[64,3,8,8,128]{4,3,2,1,0:T(8,128)(2,1)}, u32[]{:S(2)}) copy-start(bf16[64,3,8,8,128]{4,3,2,1,0:T(8,128)(2,1)} %vel.1) | copy-start | bytes 9437188
  2.5 0.9 %copy-start.1 = (bf16[256,448]{1,0:T(8,128)(2,1)S(1)}, bf16[256,448]{1,0:T(8,128)(2,1)}, u32[]{:S(2)}) copy-start(bf16[256,448]{1,0:T(8,128)(2,1)} %constant.11.clone.span_ref) | copy-start | bytes 688132
  3.5 0.9 %copy-start.2 = (bf16[128,512]{1,0:T(8,128)(2,1)S(1)}, bf16[128,512]{1,0:T(8,128)(2,1)}, u32[]{:S(2)}) copy-start(bf16[128,512]{1,0:T(8,128)(2,1)} %constant.14.clone.spread_ref) | copy-start | bytes 393220
  4.4 0.9 %copy-start.3 = (bf16[512,128]{1,0:T(8,128)(2,1)S(1)}, bf16[512,128]{1,0:T(8,128)(2,1)}, u32[]{:S(2)}) copy-start(bf16[512,128]{1,0:T(8,128)(2,1)} %constant.13.clone.fold_ref) | copy-start | bytes 393220
  5.3 0.9 %copy-start.4 = (bf16[384,128]{1,0:T(8,128)(2,1)S(1)}, bf16[384,128]{1,0:T(8,128)(2,1)}, u32[]{:S(2)}) copy-start(bf16[384,128]{1,0:T(8,128)(2,1)} %constant.12.clone.wall_ref) | copy-start | bytes 294916
  6.2 0.9 %copy-start.5 = (bf16[2,96,256]{2,1,0:T(8,128)(2,1)S(1)}, bf16[2,96,256]{2,1,0:T(8,128)(2,1)}, u32[]{:S(2)}) copy-start(bf16[2,96,256]{2,1,0:T(8,128)(2,1)} %constant.10.clone.pick_ref) | copy-start | bytes 294916
  7.1 0.7 %copy-start.6 = (f32[128]{0:T(128)S(1)}, f32[128]{0:T(128)}, u32[]{:S(2)}) copy-start(f32[128]{0:T(128)} %param.8) | copy-start | bytes 1540

commit v2 on v1

--- a/solution.py
+++ b/solution.py
@@ -77,8 +77,9 @@
 
 def kernel(
     span_count, wall_count, total_rows,
-    vel, metric_ref, pick_ref, span_ref, wall_ref, fold_ref, spread_ref,
+    vel, metric_hbm, pick_hbm, span_hbm, wall_hbm, fold_hbm, spread_hbm,
     out_ref, r_ref,
+    metric_ref, pick_ref, span_ref, wall_ref, fold_ref, spread_ref,
     u_buf, vw_buf, send_buf, lo_buf, hi_buf, ylo_buf, yhi_buf, acc, vort, prod,
     wall_sum, span_sum,
     local_sem, hs_sem, hr_sem, ys_sem, yr_sem, ws_sem, wr_sem, ss_sem, sr_sem,
@@ -96,9 +97,25 @@
     load_u = pltpu.make_async_copy(vel.at[:, 0, pl.ds(3, planes)], u_buf, local_sem.at[0])
     load_v = pltpu.make_async_copy(vel.at[:, 1], vw_buf.at[0], local_sem.at[1])
     load_w = pltpu.make_async_copy(vel.at[:, 2], vw_buf.at[1], local_sem.at[2])
+    load_pick = pltpu.make_async_copy(pick_hbm, pick_ref, local_sem.at[3])
     load_u.start()
+    load_pick.start()
     load_v.start()
     load_w.start()
+    loads = [
+        pltpu.make_async_copy(src, dst, local_sem.at[4 + i])
+        for i, (src, dst) in enumerate(
+            (
+                (wall_hbm, wall_ref),
+                (metric_hbm, metric_ref),
+                (span_hbm, span_ref),
+                (fold_hbm, fold_ref),
+                (spread_hbm, spread_ref),
+            )
+        )
+    ]
+    for load in loads:
+        load.start()
 
     barrier = pltpu.get_barrier_semaphore()
     for d in range(1, span_count):
@@ -118,6 +135,7 @@
             value = vw_buf[c - 1, at, pl.ds(3, planes)]
         return value.astype(F32).reshape(rows, lanes).astype(BF)
 
+    load_pick.wait()
     load_u.wait()
     load_v.wait()
     for c in range(2):
@@ -126,6 +144,8 @@
             for side in range(2):
                 send_buf[side, c, k * edge : (k + 1) * edge] = dot(pick_ref[side], f).astype(BF)
     load_w.wait()
+    for load in loads:
+        load.wait()
     pl.semaphore_wait(barrier, span_count + wall_count - 2)
 
     down = lax.rem(me + span_count - 1, span_count)
@@ -355,9 +375,11 @@
             jax.ShapeDtypeStruct((snaps, 3, planes, cells, lanes), BF),
             jax.ShapeDtypeStruct((snaps, snaps), F32),
         ),
-        in_specs=[pl.BlockSpec(memory_space=pl.ANY)] + [vmem] * 6,
+        in_specs=[pl.BlockSpec(memory_space=pl.ANY)] * 7,
         out_specs=(vmem, vmem),
         scratch_shapes=[
+            pltpu.VMEM((1, lanes), F32),
+            *[pltpu.VMEM(a.shape, a.dtype) for a in consts],
             pltpu.VMEM((snaps, planes, cells, lanes), BF),
             pltpu.VMEM((2, snaps, depth, cells, lanes), BF),
             pltpu.VMEM((2, 2, edge, lanes), BF),
@@ -370,7 +392,7 @@
             pltpu.VMEM((wide // 128, wide, 128), F32),
             pltpu.VMEM((walls, snaps // 2, 2 * snaps), F32),
             pltpu.VMEM((spans, snaps // 2, 2 * snaps), F32),
-            dma((3,)),
+            dma((9,)),
             dma((2, 2)),
             dma((2, 2)),
             dma((2, 2)),
@@ -381,7 +403,7 @@
             dma((spans,)),
         ],
         compiler_params=pltpu.CompilerParams(
-            collective_id=0, has_side_effects=True, vmem_limit_bytes=48 << 20
+            collective_id=0, has_side_effects=True, vmem_limit_bytes=60 << 20
         ),
         name="pod",
     )(velocity, wall_metric.reshape(1, lanes), *consts)

time: 43.8 us -> 39.3 us (0.90)
  local copies, waits for them, and re-layouts: 8.57 us -> 3.47 us
  Pallas kernels: 34.3 us -> 34.9 us
    unnamed x16 -> x2, local copies, waits for them, and re-layouts: 8.57 us -> 3.47 us
    pallas_call x1, Pallas kernels: 34.3 us -> 34.9 us  [per_device(): pl.pallas_call(functools.partial(kernel, spans, walls, total_rows), out_s...]
where the time goes in v2:
time: 39.3 us; the launch traced here: 39 us
  Pallas kernels  34.9 us (89%)
  local copies, waits for them, and re-layouts  3.47 us (9%)
  between operations  0.64 us (2%)
    pallas_call x1, Pallas kernels, per_device(): pl.pallas_call(functools.partial(kernel, spans, walls, total_rows), out_s...  34.9 us
    unnamed x2, local copies, waits for them, and re-layouts  3.47 us

profile of v2, /device:TPU:0, one launch (start us, length us, event | category | flops | bytes accessed | tf_op | source)
XLA Modules:
  0.0 39.0 jit_solution(4240230571830334342)
XLA Ops:
  0.6 34.9 %pod.1 = (bf16[64,3,2,8,128]{4,3,2,1,0:T(8,128)(2,1)}, f32[64,64]{1,0:T(8,128)}) custom-call(bf16[64,3,8,8,128]{4,3,2,1,0:T(8,128)(2,1)} %vel.1, f32[1,128]{1,0:T(1,128)} %bitcast.1, bf16[2,96,256]{2,1,0:T(8,128)(2,1)} %constant.10.clone.pick_hbm, bf16[256,448]{1,0:T(8,128)(2,1)} %constant.11.clone.span_hbm, bf16[384,128]{1,0:T(8,128)(2,1)} %constant.12.clone.wall_hbm, ...), custom_call_target="tpu_custom_call" | custom-call | tf_op jit(solution)/shard_map/pod/pallas_call | solution.py:372
  35.6 2.1 %copy.11 = bf16[64,3,2,8,128]{4,3,2,1,0:T(8,128)(2,1)} copy(bf16[64,3,2,8,128]{4,3,2,1,0:T(8,128)(2,1)} %get-tuple-element.4) | data formatting | bytes 1572864
  37.7 1.4 %copy.12 = f32[64,64]{1,0:T(8,128)} copy(f32[64,64]{1,0:T(8,128)} %get-tuple-element.5) | data formatting | bytes 32768

commit v3 on v2

--- a/solution.py
+++ b/solution.py
@@ -44,12 +44,24 @@
     )
     y = np.arange(lanes)
     diff = y[:, None] - y[None, :]
-    wall = np.concatenate([coef(diff), coef(diff - lanes), coef(diff + lanes)], axis=0)
+    wall = coef(diff)
+    packs = 2 * snaps // block
+    step = lanes // packs
+    gather = np.zeros((packs, lanes, lanes), np.float32)
+    scatter = np.zeros((2, lanes, packs, lanes), np.float32)
+    for g in range(packs):
+        for t in range(3):
+            gather[g, t, g * step + t] = 1.0
+            gather[g, lanes - 3 + t, g * step + 3 + t] = 1.0
+            scatter[0, g * step + 3 + t, g] = coef(t - 3 - y)
+            scatter[1, g * step + t, g] = coef(lanes + t - y)
+    gather = gather.reshape(packs * lanes, lanes)
+    scatter = scatter.reshape(2 * lanes, packs * lanes)
     owner = np.arange(snaps * cells) // cells
     one = (owner[:, None] == np.arange(snaps)[None, :]).astype(np.float32)
     fold = np.concatenate([one, one], axis=1)
     spread = np.concatenate([np.zeros_like(one.T), one.T], axis=0)
-    return [jnp.asarray(a.astype(ml_dtypes.bfloat16)) for a in (pick, span, wall, fold, spread)]
+    return [jnp.asarray(a.astype(ml_dtypes.bfloat16)) for a in (pick, gather, span, wall, scatter, fold, spread)]
 
 
 def dot(a, b):
@@ -60,29 +72,48 @@
     groups = list(rows)
     count = len(groups)
     sub = lax.broadcasted_iota(jnp.int32, (8, 128), 0)
-    for j in range(8 * count):
-        b, r = divmod(j, 8)
-        pivot_row = jnp.broadcast_to(groups[b][r : r + 1, :], (8, 128))
-        inv = 1.0 / jnp.broadcast_to(pivot_row[:, j : j + 1], (8, 128))
-        scaled = pivot_row * inv
-        for i in range(b, count):
-            if i == b and r == 7:
-                continue
-            column = jnp.broadcast_to(groups[i][:, j : j + 1], (8, 128))
-            if i == b:
-                column = jnp.where(sub > r, column, 0.0)
-            groups[i] = groups[i] - column * scaled
+
+    def wide(value):
+        return jnp.broadcast_to(value, (8, 128))
+
+    for b in range(count):
+        at = 8 * b
+        p = [wide(groups[b][k : k + 1, :]) for k in range(8)]
+        s = {(k, l): wide(p[k][:, at + l : at + l + 1]) for k in range(8) for l in range(k, 8)}
+        inv, f = [], {}
+        for k in range(8):
+            inv.append(1.0 / s[k, k])
+            for l in range(k + 1, 8):
+                f[k, l] = s[k, l] * inv[k]
+                for m in range(l, 8):
+                    s[l, m] = s[l, m] - f[k, l] * s[k, m]
+        for k in range(8):
+            for l in range(k + 1, 8):
+                p[l] = p[l] - f[k, l] * p[k]
+        scaled = [p[k] * inv[k] for k in range(8)]
+        for i in range(b + 1, count):
+            c = [wide(groups[i][:, at + k : at + k + 1]) for k in range(8)]
+            value = groups[i]
+            for k in range(8):
+                for l in range(k + 1, 8):
+                    c[l] = c[l] - c[k] * f[k, l]
+                value = value - c[k] * scaled[k]
+            groups[i] = value
+        group = p[0]
+        for k in range(1, 8):
+            group = jnp.where(sub == k, p[k], group)
+        groups[b] = group
     return groups
 
 
 def kernel(
-    span_count, wall_count, total_rows,
-    vel, metric_hbm, pick_hbm, span_hbm, wall_hbm, fold_hbm, spread_hbm,
+    span_count, near_count, wall_count, total_rows,
+    vel, metric_hbm, pick_hbm, gather_hbm, span_hbm, wall_hbm, scatter_hbm, fold_hbm, spread_hbm,
     out_ref, r_ref,
-    metric_ref, pick_ref, span_ref, wall_ref, fold_ref, spread_ref,
-    u_buf, vw_buf, send_buf, lo_buf, hi_buf, ylo_buf, yhi_buf, acc, vort, prod,
-    wall_sum, span_sum,
-    local_sem, hs_sem, hr_sem, ys_sem, yr_sem, ws_sem, wr_sem, ss_sem, sr_sem,
+    metric_ref, pick_ref, gather_ref, span_ref, wall_ref, scatter_ref, fold_ref, spread_ref,
+    u_buf, vw_buf, send_buf, lo_buf, hi_buf, ysend_buf, ylo_buf, yhi_buf, acc, vort, prod,
+    wall_sum, far_sum, near_sum,
+    local_sem, hs_sem, hr_sem, ys_sem, yr_sem, ws_sem, wr_sem, fs_sem, fr_sem, ns_sem, nr_sem,
 ):
     snaps = vel.shape[0]
     planes = u_buf.shape[1]
@@ -106,6 +137,8 @@
         pltpu.make_async_copy(src, dst, local_sem.at[4 + i])
         for i, (src, dst) in enumerate(
             (
+                (gather_hbm, gather_ref),
+                (scatter_hbm, scatter_ref),
                 (wall_hbm, wall_ref),
                 (metric_hbm, metric_ref),
                 (span_hbm, span_ref),
@@ -118,10 +151,22 @@
         load.start()
 
     barrier = pltpu.get_barrier_semaphore()
-    for d in range(1, span_count):
-        pl.semaphore_signal(
-            barrier, inc=1, device_id=(lax.rem(me + d, span_count), mw), device_id_type=MESH
-        )
+    far_count = span_count // near_count
+    near, far = lax.rem(me, near_count), me // near_count
+
+    def near_peer(d):
+        return far * near_count + lax.rem(near + d, near_count)
+
+    def far_peer(d):
+        return lax.rem(far + d, far_count) * near_count + near
+
+    down = lax.rem(me + span_count - 1, span_count)
+    up = lax.rem(me + 1, span_count)
+    peers = [down, up]
+    peers += [near_peer(d) for d in range(1, near_count)]
+    peers += [far_peer(d) for d in range(1, far_count)]
+    for peer in peers:
+        pl.semaphore_signal(barrier, inc=1, device_id=(peer, mw), device_id_type=MESH)
     for d in range(1, wall_count):
         pl.semaphore_signal(
             barrier, inc=1, device_id=(me, lax.rem(mw + d, wall_count)), device_id_type=MESH
@@ -146,10 +191,12 @@
     load_w.wait()
     for load in loads:
         load.wait()
-    pl.semaphore_wait(barrier, span_count + wall_count - 2)
-
-    down = lax.rem(me + span_count - 1, span_count)
-    up = lax.rem(me + 1, span_count)
+    ysend_buf[...] = dot(
+        jnp.concatenate([inner(2 * c, k) for c in range(2) for k in range(blocks)], axis=1),
+        gather_ref[...],
+    ).astype(BF)
+    pl.semaphore_wait(barrier, len(peers) + wall_count - 1)
+
     halo = []
     for c in range(2):
         to_down = pltpu.make_async_remote_copy(
@@ -164,31 +211,22 @@
         to_up.start()
         halo.append((to_down, to_up))
 
-    wall_src = (u_buf, vw_buf.at[1, :, pl.ds(3, planes)])
-    y_up = [
-        pltpu.make_async_remote_copy(
-            wall_src[c], ylo_buf.at[c], ys_sem.at[0, c], yr_sem.at[0, c],
-            device_id=(me, lax.rem(mw + 1, wall_count)), device_id_type=MESH,
-        )
-        for c in range(2)
-    ]
-    y_down = [
-        pltpu.make_async_remote_copy(
-            wall_src[c], yhi_buf.at[c], ys_sem.at[1, c], yr_sem.at[1, c],
-            device_id=(me, lax.rem(mw + wall_count - 1, wall_count)), device_id_type=MESH,
-        )
-        for c in range(2)
-    ]
+    y_up = pltpu.make_async_remote_copy(
+        ysend_buf, ylo_buf, ys_sem.at[0], yr_sem.at[0],
+        device_id=(me, lax.rem(mw + 1, wall_count)), device_id_type=MESH,
+    )
+    y_down = pltpu.make_async_remote_copy(
+        ysend_buf, yhi_buf, ys_sem.at[1], yr_sem.at[1],
+        device_id=(me, lax.rem(mw + wall_count - 1, wall_count)), device_id_type=MESH,
+    )
 
     @pl.when(mw < wall_count - 1)
     def _():
-        for c in range(2):
-            y_up[c].start()
+        y_up.start()
 
     @pl.when(mw > 0)
     def _():
-        for c in range(2):
-            y_down[c].start()
+        y_down.start()
 
     @pl.when(mw == 0)
     def _():
@@ -217,22 +255,20 @@
 
     @pl.when(mw > 0)
     def _():
-        for c in range(2):
-            y_up[c].wait_recv()
+        y_up.wait_recv()
 
     @pl.when(mw < wall_count - 1)
     def _():
-        for c in range(2):
-            y_down[c].wait_recv()
-
+        y_down.wait_recv()
+
+    sides = jnp.concatenate([ylo_buf[...], yhi_buf[...]], axis=1)
     metric = metric_ref[...].reshape(1, 1, 1, lanes)
     for c in range(2):
         for k in range(blocks):
             at = pl.ds(k * block, block)
             f = inner(2 * c, k)
-            low = ylo_buf[c, at].astype(F32).reshape(rows, lanes).astype(BF)
-            high = yhi_buf[c, at].astype(F32).reshape(rows, lanes).astype(BF)
-            d = dot(jnp.concatenate([f, low, high], axis=1), wall_ref[...])
+            g = c * blocks + k
+            d = dot(f, wall_ref[...]) + dot(sides, scatter_ref[:, g * lanes : (g + 1) * lanes])
             d = d.reshape(block, planes, cells, lanes) * metric
             for p in range(planes):
                 if c == 0:
@@ -288,33 +324,36 @@
     lane = lax.broadcasted_iota(jnp.int32, (half, 2 * snaps), 1)
     packed = jnp.where(lane < snaps, g[:half], g[half:])
 
-    wall_sum[mw] = packed
     copies = []
-    for d in range(1, wall_count):
-        copy = pltpu.make_async_remote_copy(
-            wall_sum.at[mw], wall_sum.at[mw], ws_sem.at[d], wr_sem.at[d],
-            device_id=(me, lax.rem(mw + d, wall_count)), device_id_type=MESH,
-        )
-        copy.start()
-        copies.append(copy)
-    for copy in copies:
-        copy.wait_recv()
-    total = wall_sum[0]
-    for i in range(1, wall_count):
-        total = total + wall_sum[i]
-    span_sum[me] = total
-    for d in range(1, span_count):
-        copy = pltpu.make_async_remote_copy(
-            span_sum.at[me], span_sum.at[me], ss_sem.at[d], sr_sem.at[d],
-            device_id=(lax.rem(me + d, span_count), mw), device_id_type=MESH,
-        )
-        copy.start()
-        copies.append(copy)
-    for copy in copies[wall_count - 1 :]:
-        copy.wait_recv()
-    total = span_sum[0]
-    for i in range(1, span_count):
-        total = total + span_sum[i]
+
+    def gather_sum(value, buf, mine, count, send, recv, device):
+        buf[mine] = value
+        started = []
+        for d in range(1, count):
+            copy = pltpu.make_async_remote_copy(
+                buf.at[mine], buf.at[mine], send.at[d], recv.at[d],
+                device_id=device(d), device_id_type=MESH,
+            )
+            copy.start()
+            started.append(copy)
+        for copy in started:
+            copy.wait_recv()
+        copies.extend(started)
+        total = buf[0]
+        for i in range(1, count):
+            total = total + buf[i]
+        return total
+
+    total = gather_sum(
+        packed, wall_sum, mw, wall_count, ws_sem, wr_sem,
+        lambda d: (me, lax.rem(mw + d, wall_count)),
+    )
+    total = gather_sum(
+        total, far_sum, far, far_count, fs_sem, fr_sem, lambda d: (far_peer(d), mw)
+    )
+    total = gather_sum(
+        total, near_sum, near, near_count, ns_sem, nr_sem, lambda d: (near_peer(d), mw)
+    )
     gram = total / total_rows
 
     sub = lax.broadcasted_iota(jnp.int32, (half, 2 * snaps), 0)
@@ -350,19 +389,21 @@
 
     @pl.when(mw < wall_count - 1)
     def _():
-        for c in range(2):
-            y_up[c].wait_send()
+        y_up.wait_send()
 
     @pl.when(mw > 0)
     def _():
-        for c in range(2):
-            y_down[c].wait_send()
+        y_down.wait_send()
 
 
 def per_device(velocity, wall_metric):
     snaps, comps, depth, cells, lanes = velocity.shape
     planes = depth - 6
     spans, walls = lax.axis_size("span"), lax.axis_size("wall")
+    near = 1
+    while spans % (2 * near) == 0 and 4 * near * near <= spans:
+        near *= 2
+    far = spans // near
     total_rows = 3 * planes * cells * spans * lanes * walls
     consts = constants(snaps, cells, lanes, planes, 16)
     vmem = pl.BlockSpec(memory_space=pltpu.VMEM)
@@ -370,12 +411,12 @@
     edge = snaps * planes * 3
     wide = snaps * cells
     return pl.pallas_call(
-        functools.partial(kernel, spans, walls, total_rows),
+        functools.partial(kernel, spans, near, walls, total_rows),
         out_shape=(
             jax.ShapeDtypeStruct((snaps, 3, planes, cells, lanes), BF),
             jax.ShapeDtypeStruct((snaps, snaps), F32),
         ),
-        in_specs=[pl.BlockSpec(memory_space=pl.ANY)] * 7,
+        in_specs=[pl.BlockSpec(memory_space=pl.ANY)] * (2 + len(consts)),
         out_specs=(vmem, vmem),
         scratch_shapes=[
             pltpu.VMEM((1, lanes), F32),
@@ -385,22 +426,26 @@
             pltpu.VMEM((2, 2, edge, lanes), BF),
             pltpu.VMEM((2, edge, lanes), BF),
             pltpu.VMEM((2, edge, lanes), BF),
-            pltpu.VMEM((2, snaps, planes, cells, lanes), BF),
-            pltpu.VMEM((2, snaps, planes, cells, lanes), BF),
+            pltpu.VMEM((16 * planes * cells, lanes), BF),
+            pltpu.VMEM((16 * planes * cells, lanes), BF),
+            pltpu.VMEM((16 * planes * cells, lanes), BF),
             pltpu.VMEM((3, planes, snaps, cells, lanes), F32),
             pltpu.VMEM((wide, 3 * planes * lanes), BF),
             pltpu.VMEM((wide // 128, wide, 128), F32),
             pltpu.VMEM((walls, snaps // 2, 2 * snaps), F32),
-            pltpu.VMEM((spans, snaps // 2, 2 * snaps), F32),
-            dma((9,)),
+            pltpu.VMEM((far, snaps // 2, 2 * snaps), F32),
+            pltpu.VMEM((near, snaps // 2, 2 * snaps), F32),
+            dma((11,)),
             dma((2, 2)),
             dma((2, 2)),
-            dma((2, 2)),
-            dma((2, 2)),
+            dma((2,)),
+            dma((2,)),
             dma((walls,)),
             dma((walls,)),
-            dma((spans,)),
-            dma((spans,)),
+            dma((far,)),
+            dma((far,)),
+            dma((near,)),
+            dma((near,)),
         ],
         compiler_params=pltpu.CompilerParams(
             collective_id=0, has_side_effects=True, vmem_limit_bytes=60 << 20

time: 39.3 us -> 34 us (0.87)
  Pallas kernels: 34.9 us -> 29.6 us
    pallas_call x1, Pallas kernels: 34.9 us -> 29.6 us  [per_device(): pl.pallas_call(functools.partial(kernel, spans, near, walls, total_rows),...]
where the time goes in v3:
time: 34 us; the launch traced here: 33.7 us
  Pallas kernels  29.6 us (87%)
  local copies, waits for them, and re-layouts  3.47 us (10%)
  between operations  0.64 us (2%)
    pallas_call x1, Pallas kernels, per_device(): pl.pallas_call(functools.partial(kernel, spans, near, walls, total_rows),...  29.6 us
    unnamed x2, local copies, waits for them, and re-layouts  3.47 us

profile of v3, /device:TPU:0, one launch (start us, length us, event | category | flops | bytes accessed | tf_op | source)
XLA Modules:
  0.0 33.7 jit_solution(13292592663893105826)
XLA Ops:
  0.6 29.6 %pod.1 = (bf16[64,3,2,8,128]{4,3,2,1,0:T(8,128)(2,1)}, f32[64,64]{1,0:T(8,128)}) custom-call(bf16[64,3,8,8,128]{4,3,2,1,0:T(8,128)(2,1)} %vel.1, f32[1,128]{1,0:T(1,128)} %bitcast.1, bf16[2,96,256]{2,1,0:T(8,128)(2,1)} %constant.14.clone.pick_hbm, bf16[1024,128]{1,0:T(8,128)(2,1)} %constant.15.clone.gather_hbm, bf16[256,448]{1,0:T(8,128)(2,1)} %constant.16.clone.span_hbm, ...), custom_call_target="tpu_custom_call" | custom-call | tf_op jit(solution)/shard_map/pod/pallas_call | solution.py:413
  30.3 2.1 %copy.13 = bf16[64,3,2,8,128]{4,3,2,1,0:T(8,128)(2,1)} copy(bf16[64,3,2,8,128]{4,3,2,1,0:T(8,128)(2,1)} %get-tuple-element.4) | data formatting | bytes 1572864
  32.4 1.4 %copy.14 = f32[64,64]{1,0:T(8,128)} copy(f32[64,64]{1,0:T(8,128)} %get-tuple-element.5) | data formatting | bytes 32768

commit v4 on v3

--- a/solution.py
+++ b/solution.py
@@ -109,9 +109,9 @@
 def kernel(
     span_count, near_count, wall_count, total_rows,
     vel, metric_hbm, pick_hbm, gather_hbm, span_hbm, wall_hbm, scatter_hbm, fold_hbm, spread_hbm,
-    out_ref, r_ref,
+    vort, done_ref,
     metric_ref, pick_ref, gather_ref, span_ref, wall_ref, scatter_ref, fold_ref, spread_ref,
-    u_buf, vw_buf, send_buf, lo_buf, hi_buf, ysend_buf, ylo_buf, yhi_buf, acc, vort, prod,
+    u_buf, vw_buf, send_buf, lo_buf, hi_buf, ysend_buf, ylo_buf, yhi_buf, acc, prod,
     wall_sum, far_sum, near_sum,
     local_sem, hs_sem, hr_sem, ys_sem, yr_sem, ws_sem, wr_sem, fs_sem, fr_sem, ns_sem, nr_sem,
 ):
@@ -368,32 +368,38 @@
     sub = lax.broadcasted_iota(jnp.int32, (snaps, 2 * snaps), 0)
     diagonal = jnp.sum(jnp.where(lane == sub, done, 0.0), axis=1, keepdims=True)
     done = jnp.where(lane < sub, 0.0, done / jnp.sqrt(diagonal))
+    done_ref[...] = done
+
+    for copy in copies:
+        copy.wait_send()
+    for pair in halo:
+        for copy in pair:
+            copy.wait_send()
+
+    @pl.when(mw < wall_count - 1)
+    def _():
+        y_up.wait_send()
+
+    @pl.when(mw > 0)
+    def _():
+        y_down.wait_send()
+
+
+def modes_kernel(vort, done_ref, fold_ref, spread_ref, out_ref, r_ref):
+    snaps, comps, planes, cells, lanes = out_ref.shape
+    wide = snaps * cells
+    done = done_ref[...]
     r_ref[...] = done[:, :snaps]
-
     x = dot(done.astype(BF), spread_ref[...]).astype(BF)
     full = dot(fold_ref[:, :snaps], x)
     row_z = lax.rem(lax.broadcasted_iota(jnp.int32, (wide, wide), 0), cells)
     col_z = lax.rem(lax.broadcasted_iota(jnp.int32, (wide, wide), 1), cells)
     weights = jnp.where(row_z == col_z, full, 0.0).astype(BF)
-    for comp in range(3):
+    for comp in range(comps):
         for p in range(planes):
             slab = comp * planes + p
             m = dot(weights, vort[:, slab * lanes : (slab + 1) * lanes])
             out_ref[:, comp, p] = m.reshape(snaps, cells, lanes).astype(BF)
-
-    for copy in copies:
-        copy.wait_send()
-    for pair in halo:
-        for copy in pair:
-            copy.wait_send()
-
-    @pl.when(mw < wall_count - 1)
-    def _():
-        y_up.wait_send()
-
-    @pl.when(mw > 0)
-    def _():
-        y_down.wait_send()
 
 
 def per_device(velocity, wall_metric):
@@ -410,11 +416,11 @@
     dma = pltpu.SemaphoreType.DMA
     edge = snaps * planes * 3
     wide = snaps * cells
-    return pl.pallas_call(
+    vorticity, done = pl.pallas_call(
         functools.partial(kernel, spans, near, walls, total_rows),
         out_shape=(
-            jax.ShapeDtypeStruct((snaps, 3, planes, cells, lanes), BF),
-            jax.ShapeDtypeStruct((snaps, snaps), F32),
+            jax.ShapeDtypeStruct((wide, 3 * planes * lanes), BF),
+            jax.ShapeDtypeStruct((snaps, 2 * snaps), F32),
         ),
         in_specs=[pl.BlockSpec(memory_space=pl.ANY)] * (2 + len(consts)),
         out_specs=(vmem, vmem),
@@ -430,7 +436,6 @@
             pltpu.VMEM((16 * planes * cells, lanes), BF),
             pltpu.VMEM((16 * planes * cells, lanes), BF),
             pltpu.VMEM((3, planes, snaps, cells, lanes), F32),
-            pltpu.VMEM((wide, 3 * planes * lanes), BF),
             pltpu.VMEM((wide // 128, wide, 128), F32),
             pltpu.VMEM((walls, snaps // 2, 2 * snaps), F32),
             pltpu.VMEM((far, snaps // 2, 2 * snaps), F32),
@@ -452,6 +457,16 @@
         ),
         name="pod",
     )(velocity, wall_metric.reshape(1, lanes), *consts)
+    return pl.pallas_call(
+        modes_kernel,
+        out_shape=(
+            jax.ShapeDtypeStruct((snaps, 3, planes, cells, lanes), BF),
+            jax.ShapeDtypeStruct((snaps, snaps), F32),
+        ),
+        in_specs=[vmem] * 4,
+        out_specs=(vmem, vmem),
+        name="modes",
+    )(vorticity, done, *consts[-2:])
 
 
 def solution(mesh):

time: 34 us -> 32.5 us (0.956)
  local copies, waits for them, and re-layouts: 3.47 us -> 0 us
  Pallas kernels: 29.6 us -> 31.8 us
    unnamed x2 -> x0, local copies, waits for them, and re-layouts: 3.47 us -> none
    pallas_call x0 -> x1, Pallas kernels: none -> 3.32 us  [per_device(): pl.pallas_call(modes_kernel, out_shape=(jax.ShapeDtypeStruct((snaps, 3, p...]
    pallas_call x1, Pallas kernels: 29.6 us -> 28.4 us  [per_device(): pl.pallas_call(functools.partial(kernel, spans, near, walls, total_rows),...]
where the time goes in v4:
time: 32.5 us; the launch traced here: 32.4 us
  Pallas kernels  31.8 us (98%)
  between operations  0.64 us (2%)
    pallas_call x1, Pallas kernels, per_device(): pl.pallas_call(functools.partial(kernel, spans, near, walls, total_rows),...  28.4 us
    pallas_call x1, Pallas kernels, per_device(): pl.pallas_call(modes_kernel, out_shape=(jax.ShapeDtypeStruct((snaps, 3, p...  3.32 us

profile of v4, /device:TPU:0, one launch (start us, length us, event | category | flops | bytes accessed | tf_op | source)
XLA Modules:
  0.0 32.4 jit_solution(14699626019980989432)
XLA Ops:
  0.6 28.4 %pod.1 = (bf16[512,768]{1,0:T(8,128)(2,1)}, f32[64,128]{1,0:T(8,128)}) custom-call(bf16[64,3,8,8,128]{4,3,2,1,0:T(8,128)(2,1)} %vel.1, f32[1,128]{1,0:T(1,128)} %bitcast.1, bf16[2,96,256]{2,1,0:T(8,128)(2,1)} %constant.14.clone.pick_hbm, bf16[1024,128]{1,0:T(8,128)(2,1)} %constant.15.clone.gather_hbm, bf16[256,448]{1,0:T(8,128)(2,1)} %constant.16.clone.span_hbm, ...), custom_call_target="tpu_custom_call" | custom-call | tf_op jit(solution)/shard_map/pod/pallas_call | solution.py:419
  29.1 3.3 %modes.1 = (bf16[64,3,2,8,128]{4,3,2,1,0:T(8,128)(2,1)}, f32[64,64]{1,0:T(8,128)}) custom-call(bf16[512,768]{1,0:T(8,128)(2,1)} %get-tuple-element.4.vort, f32[64,128]{1,0:T(8,128)} %get-tuple-element.5.done_ref, bf16[512,128]{1,0:T(8,128)(2,1)} %constant.19.clone.fold_hbm.fold_ref, bf16[128,512]{1,0:T(8,128)(2,1)} %constant.20.clone.spread_hbm.spread_ref), custom_call_target="tpu_custom_call" | custom-call | tf_op jit(solution)/shard_map/modes/pallas_call | solution.py:460
